TPU v7x, 32 devices: a whole 2x2x4 slice. The times are simulated.
32 devices in a mesh: teacher: 4 (over y, x), vocab: 8 (over z, core).
Axes of the slice: x: 2, y: 2, z: 4, core: 2. Of those that a mesh axis runs over, the one named last changes fastest.
Arguments:
- teacher_hidden: bfloat16 [4, 1024, 4096], P('teacher', 'vocab'), may hold values from -180 to 180
- teacher_head: bfloat16 [4, 4096, 32000], P('teacher', None, 'vocab'), may hold values from -0.375 to 0.375
- student_hidden: bfloat16 [1024, 4096], P('teacher'), may hold values from -180 to 180
- student_head: bfloat16 [4096, 32000], P('teacher', 'vocab'), may hold values from -0.375 to 0.375
Outputs:
- loss: float32 [], replicated
- grad_hidden: float32 [1024, 4096], P('teacher', 'vocab')
- grad_weight: float32 [4096, 32000], P('teacher', 'vocab')
All inputs are finite; a program needn't handle non-finite values.
Results may differ from a plain program's by a relative error of at most 0.0027.
Values may be sent and summed in bfloat16 or wider, within the bound.
A program may use at most 192 MiB of HBM per device.

v0:
```python
import jax
import jax.numpy as jnp
from jax import lax
from jax.sharding import PartitionSpec as P

TOK = 1024


def teacher_stats(logits):
    local_top = jnp.max(logits, axis=-1)
    top = lax.pmax(local_top, "vocab")
    shifted = jnp.exp(logits - top[:, None])
    total, moment = lax.psum(
        (jnp.sum(shifted, axis=-1), jnp.sum(shifted * logits, axis=-1)), "vocab"
    )
    return (top, total, moment)


def paired_lse(stacked):
    local_top = jnp.max(stacked, axis=-1)
    top = lax.pmax(local_top, "vocab")
    total = lax.psum(jnp.sum(jnp.exp(stacked - top[..., None]), axis=-1), "vocab")
    return top + jnp.log(total)


def per_device(teacher_hidden, teacher_head, student_hidden, student_head):
    head = teacher_head[0]
    logits = jnp.dot(
        lax.all_gather(teacher_hidden[0], "vocab", axis=0, tiled=True),
        head,
        preferred_element_type=jnp.float32,
    )
    top, total, moment = teacher_stats(logits)
    lse = top + jnp.log(total)
    entropy = lse - moment / total
    confid = jnp.exp(-entropy)
    weighted = confid[:, None] * (logits - lse[:, None])
    wsum, csum = (
        lax.psum_scatter(weighted, "teacher", scatter_dimension=0, tiled=True),
        lax.psum_scatter(confid, "teacher", scatter_dimension=0, tiled=True),
    )
    raw = wsum / csum[:, None]
    full_head = lax.all_gather(student_head, "teacher", axis=0, tiled=True)
    slog = jnp.dot(student_hidden, full_head, preferred_element_type=jnp.float32)
    both_lse = paired_lse(jnp.stack([raw, slog]))
    target = raw - both_lse[0][:, None]
    slp = slog - both_lse[1][:, None]
    probs = jnp.exp(target)
    partial_kl = jnp.sum(probs * (target - slp))
    loss = lax.psum(partial_kl, ("teacher", "vocab")) / TOK
    gradl = (jnp.exp(slp) - probs).astype(jnp.bfloat16)
    grad_hidden = lax.psum_scatter(
        lax.dot_general(
            full_head, gradl, (((1,), (1,)), ((), ())), preferred_element_type=jnp.float32
        ),
        "vocab",
        scatter_dimension=0,
        tiled=True,
    ).T
    columns = lax.all_to_all(student_hidden, "teacher", split_axis=1, concat_axis=0, tiled=True)
    all_grads = lax.all_gather(gradl, "teacher", axis=0, tiled=True)
    grad_weight = lax.dot_general(
        columns, all_grads, (((0,), (0,)), ((), ())), preferred_element_type=jnp.float32
    )
    return (loss, grad_hidden, grad_weight)


def solution(mesh):
    placed = (
        P("teacher", "vocab", None),
        P("teacher", None, "vocab"),
        P("teacher", None),
        P("teacher", "vocab"),
    )
    return jax.shard_map(
        per_device,
        mesh=mesh,
        in_specs=placed,
        out_specs=(P(), P("teacher", "vocab"), P("teacher", "vocab")),
        check_vma=False,
    )
```

profile of v0, /device:TPU:0, one launch (start us, length us, event | category | flops | bytes accessed | tf_op | source)
XLA Modules:
  0.0 849.6 jit_solution(5529223192047300215)
XLA Ops:
  7.9 86.4 %all-gather.9.cloned.1.call-done = bf16[1,1024,4096]{2,1,0:T(8,128)(2,1)} async-done(((bf16[1,128,4096]{2,1,0:T(8,128)(2,1)}), bf16[1,1024,4096]{2,1,0:T(8,128)(2,1)}) %all-gather.9.cloned.1.call-update) | async-done | bytes 8388624 | tf_op jit(solution)/shard_map/all_gather | solution.py:29
  94.4 41.8 %fusion.7 = (f32[1024]{0:T(1024)S(1)}, f32[1024,4000]{0,1:T(8,128)}) fusion(bf16[1,4096,4000]{1,2,0:T(8,128)(2,1)} %param.5, bf16[1,1024,4096]{2,1,0:T(8,128)(2,1)} %all-gather.9.cloned.1.call-done), kind=kOutput, calls=%fused_computation.20 | convolution fusion | flops 33558528000 | bytes 57544704 | tf_op jit(solution)/shard_map/dot_general | solution.py:28
  136.2 14.0 %pmax.14 = f32[1024]{0:T(1024)S(1)} all-reduce(f32[1024]{0:T(1024)S(1)} %get-tuple-element.13), channel_id=1, replica_groups=mesh['teacher'=4,'vocab'=8] {'vocab'}, use_global_device_ids=true, to_apply=%region_1.0 | all-reduce | flops 1024 | bytes 8192 | tf_op jit(solution)/shard_map/pmax | solution.py:11
  150.2 7.6 multiply_reduce_fusion
  157.8 13.9 %all-reduce.1 = (f32[1024]{0:T(1024)S(1)}, f32[1024]{0:T(1024)S(1)}) all-reduce(f32[1024]{0:T(1024)S(1)} %get-tuple-element.4, f32[1024]{0:T(1024)S(1)} %get-tuple-element.3), channel_id=1, replica_groups=mesh['teacher'=4,'vocab'=8] {'vocab'}, use_global_device_ids=true, to_apply=%region_3.0 | all-reduce | flops 2048 | bytes 16384 | tf_op jit(solution)/shard_map/psum | solution.py:13
  171.7 11.5 %subtract_multiply_fusion = f32[1024,4000]{0,1:T(8,128)} fusion(f32[1024,4000]{0,1:T(8,128)} %get-tuple-element.14, f32[1024]{0:T(1024)S(1)} %get-tuple-element.10, f32[1024]{0:T(1024)S(1)} %get-tuple-element.9), kind=kLoop, calls=%fused_computation.2 | loop fusion | flops 8192000 | bytes 32776192 | tf_op jit(solution)/shard_map/mul | solution.py:37
  185.3 10.4 %all-reduce = f32[1024]{0:T(1024)S(1)} all-reduce(f32[1024]{0:T(1024)S(1)} %get-tuple-element.9), channel_id=4, replica_groups=mesh['teacher'=4,'vocab'=8] {'teacher'}, use_global_device_ids=true, to_apply=%region_7.0.clone | all-reduce | flops 1024 | bytes 8192
  195.8 136.6 %reduce-scatter.3.cloned.1.call-done = f32[256,4000]{0,1:T(8,128)} async-done(((f32[1024,4000]{0,1:T(8,128)}), f32[256,4000]{0,1:T(8,128)}) %reduce-scatter.3.cloned.1.call-update) | async-done | bytes 4096016 | tf_op jit(solution)/shard_map/reduce_scatter | solution.py:39
  332.4 4.4 fusion.5
  336.8 288.4 %all-gather.5.cloned.1.call-done = bf16[4096,4000]{0,1:T(8,128)(2,1)} async-done(((bf16[1024,4000]{0,1:T(8,128)(2,1)}), bf16[4096,4000]{0,1:T(8,128)(2,1)}) %all-gather.5.cloned.1.call-update) | async-done | bytes 32768016 | tf_op jit(solution)/shard_map/all_gather | solution.py:43
  625.1 14.1 %fusion.8 = f32[256,4000]{0,1:T(8,128)S(1)} fusion(bf16[256,4096]{1,0:T(8,128)(2,1)S(1)} %copy-done.2, bf16[4096,4000]{0,1:T(8,128)(2,1)} %all-gather.5.cloned.1.call-done), kind=kOutput, calls=%fused_computation.21 | convolution fusion | flops 8388608000 | bytes 38961152 | tf_op jit(solution)/shard_map/dot_general | solution.py:44
  639.3 2.0 copy-done.1
  641.8 16.3 %pmax.15 = f32[2,256]{1,0:T(2,128)S(1)} all-reduce(f32[2,256]{1,0:T(2,128)S(1)} %fusion.4), channel_id=1, replica_groups=mesh['teacher'=4,'vocab'=8] {'vocab'}, use_global_device_ids=true, to_apply=%region_9.0 | all-reduce | flops 512 | bytes 4096 | tf_op jit(solution)/shard_map/pmax | solution.py:21
  658.2 4.0 exponential_reduce_fusion
  662.1 13.8 %psum.30 = f32[2,256]{1,0:T(2,128)S(1)} all-reduce(f32[2,256]{1,0:T(2,128)S(1)} %exponential_reduce_fusion), channel_id=1, replica_groups=mesh['teacher'=4,'vocab'=8] {'vocab'}, use_global_device_ids=true, to_apply=%region_11.0 | all-reduce | flops 512 | bytes 4096 | tf_op jit(solution)/shard_map/psum | solution.py:22
  675.9 6.9 subtract_convert_fusion
  682.9 18.8 %convolution_bitcast_fusion.1 = f32[4096,256]{0,1:T(8,128)} fusion(bf16[256,4000]{0,1:T(8,128)(2,1)} %get-tuple-element.7, bf16[4096,4000]{0,1:T(8,128)(2,1)} %all-gather.5.cloned.1.call-done), kind=kOutput, calls=%fused_computation.11 | convolution fusion | flops 8388608000 | bytes 39010304 | tf_op jit(solution)/shard_map/dot_general | solution.py:53
  701.8 2.5 copy.9
  704.2 32.7 %all_to_all.19 = bf16[256,4,1024]{0,2,1:T(8,128)(2,1)S(1)} all-to-all(bf16[256,4,1024]{0,2,1:T(8,128)(2,1)} %bitcast.33), channel_id=1, replica_groups=mesh['teacher'=4,'vocab'=8] {'teacher'}, dimensions={1} | all-to-all | bytes 4194304 | tf_op jit(solution)/shard_map/all_to_all | solution.py:60
  736.9 2.5 copy.10
  739.4 40.0 %psum.31 = f32[]{:T(128)} all-reduce(f32[]{:T(128)} %get-tuple-element.8), channel_id=1, replica_groups=mesh['teacher'=4,'vocab'=8] {'teacher','vocab'}, use_global_device_ids=true, to_apply=%region_13.0 | all-reduce | flops 1 | bytes 8 | tf_op jit(solution)/shard_map/psum | solution.py:50
  780.0 9.0 %all-gather.7.cloned.1.call-done = bf16[1024,4000]{0,1:T(8,128)(2,1)} async-done(((bf16[256,4000]{0,1:T(8,128)(2,1)}), bf16[1024,4000]{0,1:T(8,128)(2,1)}) %all-gather.7.cloned.1.call-update) | async-done | bytes 8192016 | tf_op jit(solution)/shard_map/all_gather | solution.py:61
  789.1 15.9 %convolution_bitcast_fusion = f32[1024,4000]{0,1:T(8,128)} fusion(bf16[1024,4000]{0,1:T(8,128)(2,1)} %all-gather.7.cloned.1.call-done, bf16[1024,1024]{1,0:T(8,128)(2,1)} %bitcast.34), kind=kOutput, calls=%fused_computation.6 | convolution fusion | flops 8388608000 | bytes 26673152 | tf_op jit(solution)/shard_map/dot_general | solution.py:62
  804.9 37.0 %reduce-scatter.5.cloned.1.call-done = f32[512,256]{0,1:T(8,128)} async-done(((f32[4096,256]{0,1:T(8,128)}), f32[512,256]{0,1:T(8,128)}) %reduce-scatter.5.cloned.1.call-update) | async-done | bytes 524304 | tf_op jit(solution)/shard_map/reduce_scatter | solution.py:52
  (23 shorter events, 2.9 us)
Async XLA Ops:
  7.2 87.2 %all-gather.9.cloned.1.call-start = ((), (), s32[]{:S(2)}) async-start(), calls=%async_computation.7 | async-start | bytes 9437184 | tf_op jit(solution)/shard_map/all_gather | solution.py:29
  7.9 324.5 %reduce-scatter.3.cloned.1.call-start = ((), (), s32[]{:S(2)}) async-start(), calls=%async_computation.3 | async-start | bytes 20480000 | tf_op jit(solution)/shard_map/reduce_scatter | solution.py:39
  183.3 0.8 copy-start.3
  183.3 441.8 %copy-start.2 = (bf16[256,4096]{1,0:T(8,128)(2,1)S(1)}, bf16[256,4096]{1,0:T(8,128)(2,1)}, u32[]{:S(2)}) copy-start(bf16[256,4096]{1,0:T(8,128)(2,1)} %param.6) | copy-start | bytes 6291460
  183.3 441.8 %all-gather.5.cloned.1.call-start = ((), (), s32[]{:S(2)}) async-start(), calls=%async_computation.4 | async-start | bytes 40960000 | tf_op jit(solution)/shard_map/all_gather | solution.py:43
  184.0 605.0 %all-gather.7.cloned.1.call-start = ((), (), s32[]{:S(2)}) async-start(), calls=%async_computation.6 | async-start | bytes 10240000 | tf_op jit(solution)/shard_map/all_gather | solution.py:61
  625.1 16.1 %copy-start = (f32[1,256,4000]{1,2,0:T(8,128)S(1)}, f32[1,256,4000]{1,2,0:T(8,128)}, u32[]{:S(2)}) copy-start(f32[1,256,4000]{1,2,0:T(8,128)} %fusion.5) | copy-start | bytes 12288004
  639.3 2.0 copy-start.1
  682.9 159.0 %reduce-scatter.5.cloned.1.call-start = ((), (), s32[]{:S(2)}) async-start(), calls=%async_computation.5 | async-start | bytes 4718592 | tf_op jit(solution)/shard_map/reduce_scatter | solution.py:52
Sparse Core Ops, SparseCore 0:
  9.6 84.7 all-gather.8
  183.4 148.9 reduce-scatter.2
  334.4 290.6 all-gather.4
  683.0 106.0 all-gather.6
  791.9 49.9 reduce-scatter.4
where the time goes:
time: 850 us
  waiting for transfers between devices  559 us (66%)
  blocking collectives  141 us (17%)
  matrix products  90.6 us (11%)
  other arithmetic  34.9 us (4%)
  between operations  16.3 us (2%)
    all_gather x1, waiting for transfers between devices, per_device(): full_head = lax.all_gather(student_head, 'teacher', axis=0, tiled=True)  288 us
    reduce_scatter x1, waiting for transfers between devices, per_device(): lax.psum_scatter(weighted, 'teacher', scatter_dimension=0, tiled=True)  137 us
    all_gather x1, waiting for transfers between devices, per_device(): lax.all_gather(teacher_hidden[0], 'vocab', axis=0, tiled=True)  86.4 us
    dot_general x1, matrix products, per_device(): jnp.dot(lax.all_gather(teacher_hidden[0], 'vocab', axis=0, tiled=True), h...  41.8 us
    psum x1, blocking collectives, per_device(): loss = lax.psum(partial_kl, ('teacher', 'vocab')) / TOK  40 us
    reduce_scatter x1, waiting for transfers between devices, per_device(): lax.psum_scatter(lax.dot_general(full_head, gradl, (((1,), (1,)), ((), ()...  37 us
    all_to_all x1, blocking collectives, per_device(): lax.all_to_all(student_hidden, 'teacher', split_axis=1, concat_axis=0, ti...  32.7 us
    dot_general x1, matrix products, per_device(): lax.dot_general(full_head, gradl, (((1,), (1,)), ((), ())), preferred_ele...  18.8 us
  transfers between devices with their start and end apart: 5, of which 5 were waited for; matrix products, arithmetic and copies ran while one was open for 5% of the time, Pallas kernels for 0%

commit v1 on v0

--- a/solution.py
+++ b/solution.py
@@ -4,6 +4,17 @@
 from jax.sharding import PartitionSpec as P
 
 TOK = 1024
+
+
+def around_the_ring(x, axis, dim):
+    count = lax.axis_size(axis)
+    hops = [(i, (i + 1) % count) for i in range(count)]
+    parts = [x]
+    for far in range(1, count):
+        parts = [lax.ppermute(parts[0], axis, hops), *parts]
+    out = jnp.concatenate(parts, axis=dim)
+    turn = (lax.axis_index(axis) + 1) * parts[-1].shape[dim]
+    return jnp.roll(out, turn, axis=dim)
 
 
 def teacher_stats(logits):
@@ -40,7 +51,7 @@
         lax.psum_scatter(confid, "teacher", scatter_dimension=0, tiled=True),
     )
     raw = wsum / csum[:, None]
-    full_head = lax.all_gather(student_head, "teacher", axis=0, tiled=True)
+    full_head = around_the_ring(student_head, "teacher", 0)
     slog = jnp.dot(student_hidden, full_head, preferred_element_type=jnp.float32)
     both_lse = paired_lse(jnp.stack([raw, slog]))
     target = raw - both_lse[0][:, None]

time: 850 us -> 1140 us (1.34)
  blocking collectives: 141 us -> 300 us
  waiting for transfers between devices: 559 us -> 632 us
  local copies, waits for them, and re-layouts: 7.62 us -> 67.7 us
    ppermute x0 -> x3, waiting for transfers between devices: none -> 486 us  [around_the_ring(): parts = [lax.ppermute(parts[0], axis, hops), *parts]]
    all_gather x1 -> x0, waiting for transfers between devices: 288 us -> none  [per_device(): full_head = lax.all_gather(student_head, 'teacher', axis=0, tiled=True)]
    unnamed x1, blocking collectives: 10.4 us -> 178 us
    reduce_scatter x1, waiting for transfers between devices: 137 us -> 0.01 us  [per_device(): lax.psum_scatter(weighted, 'teacher', scatter_dimension=0, tiled=True)]
    unnamed x11 -> x25, local copies, waits for them, and re-layouts: 5.11 us -> 61.1 us
    all_gather x1, waiting for transfers between devices: 9.04 us -> 58.4 us  [per_device(): all_grads = lax.all_gather(gradl, 'teacher', axis=0, tiled=True)]
    reduce_scatter x1, waiting for transfers between devices: 37 us -> 0.02 us  [per_device(): lax.psum_scatter(lax.dot_general(full_head, gradl, (((1,), (1,)), ((), ()...]
  transfers between devices with their start and end apart: 5 -> 7, of which waited for: 5 -> 4; matrix products, arithmetic and copies ran while one was open for 5% -> 7% of each run, Pallas kernels for 0% -> 0%
where the time goes in v1:
time: 1140 us
  waiting for transfers between devices  632 us (55%)
  blocking collectives  300 us (26%)
  matrix products  92.9 us (8%)
  local copies, waits for them, and re-layouts  67.7 us (6%)
  other arithmetic  31.8 us (3%)
  between operations  16.3 us (1%)
    ppermute x3, waiting for transfers between devices, around_the_ring(): parts = [lax.ppermute(parts[0], axis, hops), *parts]  486 us
    unnamed x1, blocking collectives  178 us
    all_gather x1, waiting for transfers between devices, per_device(): lax.all_gather(teacher_hidden[0], 'vocab', axis=0, tiled=True)  86.4 us
    unnamed x25, local copies, waits for them, and re-layouts  61.1 us
    all_gather x1, waiting for transfers between devices, per_device(): all_grads = lax.all_gather(gradl, 'teacher', axis=0, tiled=True)  58.4 us
    dot_general x1, matrix products, per_device(): jnp.dot(lax.all_gather(teacher_hidden[0], 'vocab', axis=0, tiled=True), h...  41.8 us
    psum x1, blocking collectives, per_device(): loss = lax.psum(partial_kl, ('teacher', 'vocab')) / TOK  37.6 us
    all_to_all x1, blocking collectives, per_device(): lax.all_to_all(student_hidden, 'teacher', split_axis=1, concat_axis=0, ti...  29 us
  transfers between devices with their start and end apart: 7, of which 4 were waited for; matrix products, arithmetic and copies ran while one was open for 7% of the time, Pallas kernels for 0%

profile of v1, /device:TPU:0, one launch (start us, length us, event | category | flops | bytes accessed | tf_op | source)
XLA Modules:
  0.0 1144.0 jit_solution(2261004604023277859)
XLA Ops:
  7.9 86.4 %all-gather.6.cloned.1.call-done = bf16[1,1024,4096]{2,1,0:T(8,128)(2,1)} async-done(((bf16[1,128,4096]{2,1,0:T(8,128)(2,1)}), bf16[1,1024,4096]{2,1,0:T(8,128)(2,1)}) %all-gather.6.cloned.1.call-update) | async-done | bytes 8388624 | tf_op jit(solution)/shard_map/all_gather | solution.py:40
  94.4 41.8 %fusion.13 = (f32[1024]{0:T(1024)S(1)}, f32[1024,4000]{0,1:T(8,128)}) fusion(bf16[1,4096,4000]{1,2,0:T(8,128)(2,1)} %param.5, bf16[1,1024,4096]{2,1,0:T(8,128)(2,1)} %all-gather.6.cloned.1.call-done), kind=kOutput, calls=%fused_computation.34 | convolution fusion | flops 33558528000 | bytes 57544704 | tf_op jit(solution)/shard_map/dot_general | solution.py:39
  136.2 14.0 %pmax.14 = f32[1024]{0:T(1024)S(1)} all-reduce(f32[1024]{0:T(1024)S(1)} %get-tuple-element.25), channel_id=1, replica_groups=mesh['teacher'=4,'vocab'=8] {'vocab'}, use_global_device_ids=true, to_apply=%region_1.0 | all-reduce | flops 1024 | bytes 8192 | tf_op jit(solution)/shard_map/pmax | solution.py:22
  150.2 7.6 multiply_reduce_fusion
  157.8 13.9 %all-reduce.1 = (f32[1024]{0:T(1024)S(1)}, f32[1024]{0:T(1024)S(1)}) all-reduce(f32[1024]{0:T(1024)S(1)} %get-tuple-element.16, f32[1024]{0:T(1024)S(1)} %get-tuple-element.15), channel_id=1, replica_groups=mesh['teacher'=4,'vocab'=8] {'vocab'}, use_global_device_ids=true, to_apply=%region_3.0 | all-reduce | flops 2048 | bytes 16384 | tf_op jit(solution)/shard_map/psum | solution.py:24
  171.7 11.5 %subtract_multiply_fusion = f32[1024,4000]{0,1:T(8,128)} fusion(f32[1024,4000]{0,1:T(8,128)} %get-tuple-element.26, f32[1024]{0:T(1024)S(1)} %get-tuple-element.22, f32[1024]{0:T(1024)S(1)} %get-tuple-element.21), kind=kLoop, calls=%fused_computation.6 | loop fusion | flops 8192000 | bytes 32776192 | tf_op jit(solution)/shard_map/mul | solution.py:48
  185.1 309.0 %collective-permute-done = bf16[1024,4000]{0,1:T(8,128)(2,1)S(1)} collective-permute-done((bf16[1024,4000]{0,1:T(8,128)(2,1)}, bf16[1024,4000]{0,1:T(8,128)(2,1)S(1)}, u32[]{:S(2)}, u32[]{:S(2)}) %collective-permute-start) | collective-permute-done | bytes 8192032 | tf_op jit(solution)/shard_map/ppermute | solution.py:14
  498.1 177.2 %collective-permute-done.1 = bf16[1024,4000]{0,1:T(8,128)(2,1)} collective-permute-done((bf16[1024,4000]{0,1:T(8,128)(2,1)S(1)}, bf16[1024,4000]{0,1:T(8,128)(2,1)}, u32[]{:S(2)}, u32[]{:S(2)}) %collective-permute-start.1) | collective-permute-done | bytes 8192032 | tf_op jit(solution)/shard_map/ppermute | solution.py:14
  676.6 178.3 %all-reduce = f32[1024]{0:T(1024)S(1)} all-reduce(f32[1024]{0:T(1024)S(1)} %get-tuple-element.21), channel_id=4, replica_groups=mesh['teacher'=4,'vocab'=8] {'teacher'}, use_global_device_ids=true, to_apply=%region_7.0.clone | all-reduce | flops 1024 | bytes 8192
  854.9 7.4 constant_dynamic-update-slice_fusion.7
  862.4 7.6 constant_dynamic-update-slice_fusion.6
  870.0 7.6 constant_dynamic-update-slice_fusion.5
  881.7 7.4 constant_dynamic-update-slice_fusion.3
  889.2 7.4 constant_dynamic-update-slice_fusion.2
  896.6 7.4 constant_dynamic-update-slice_fusion.1
  908.1 17.1 %fusion.4 = f32[4000,256]{1,0:T(8,128)} fusion(bf16[256,4096]{1,0:T(8,128)(2,1)} %param.6, bf16[8192,4000]{0,1:T(8,128)(2,1)} %constant_dynamic-update-slice_fusion, s32[]{:T(128)S(6)} %select_n.14), kind=kOutput, calls=%fused_computation.4 | convolution fusion | flops 8388608000 | bytes 38961156 | tf_op jit(solution)/shard_map/dot_general | solution.py:55
  930.4 13.6 %pmax.15 = f32[2,256]{1,0:T(2,128)S(1)} all-reduce(f32[2,256]{1,0:T(2,128)S(1)} %fusion.8), channel_id=1, replica_groups=mesh['teacher'=4,'vocab'=8] {'vocab'}, use_global_device_ids=true, to_apply=%region_9.10 | all-reduce | flops 512 | bytes 4096 | tf_op jit(solution)/shard_map/pmax | solution.py:32
  947.9 13.9 %psum.30 = f32[2,256]{1,0:T(2,128)S(1)} all-reduce(f32[2,256]{1,0:T(2,128)S(1)} %exponential_reduce_fusion), channel_id=1, replica_groups=mesh['teacher'=4,'vocab'=8] {'vocab'}, use_global_device_ids=true, to_apply=%region_11.12 | all-reduce | flops 512 | bytes 4096 | tf_op jit(solution)/shard_map/psum | solution.py:33
  961.8 5.6 subtract_convert_fusion
  967.4 18.1 %fusion.2 = f32[4096,256]{1,0:T(8,128)} fusion(bf16[256,4000]{0,1:T(8,128)(2,1)S(1)} %get-tuple-element.19, bf16[8192,4000]{0,1:T(8,128)(2,1)} %constant_dynamic-update-slice_fusion, s32[]{:T(128)S(6)} %select_n.14), kind=kOutput, calls=%fused_computation.2 | convolution fusion | flops 8388608000 | bytes 39010308 | tf_op jit(solution)/shard_map/dot_general | solution.py:64
  990.2 29.0 %all_to_all.19 = bf16[256,4,1024]{0,2,1:T(8,128)(2,1)S(1)} all-to-all(bf16[256,4,1024]{0,2,1:T(8,128)(2,1)} %bitcast.38), channel_id=1, replica_groups=mesh['teacher'=4,'vocab'=8] {'teacher'}, dimensions={1} | all-to-all | bytes 4194304 | tf_op jit(solution)/shard_map/all_to_all | solution.py:71
  1021.8 37.6 %psum.31 = f32[]{:T(128)} all-reduce(f32[]{:T(128)} %get-tuple-element.20), channel_id=1, replica_groups=mesh['teacher'=4,'vocab'=8] {'teacher','vocab'}, use_global_device_ids=true, to_apply=%region_13.14 | all-reduce | flops 1 | bytes 8 | tf_op jit(solution)/shard_map/psum | solution.py:61
  1062.1 58.4 %all-gather.4.cloned.1.call-done = bf16[1024,4000]{0,1:T(8,128)(2,1)} async-done(((bf16[256,4000]{0,1:T(8,128)(2,1)}), bf16[1024,4000]{0,1:T(8,128)(2,1)}) %all-gather.4.cloned.1.call-update) | async-done | bytes 8192016 | tf_op jit(solution)/shard_map/all_gather | solution.py:72
  1120.5 15.9 %convolution_bitcast_fusion = f32[1024,4000]{0,1:T(8,128)} fusion(bf16[1024,4000]{0,1:T(8,128)(2,1)} %all-gather.4.cloned.1.call-done, bf16[1024,1024]{1,0:T(8,128)(2,1)} %bitcast.39), kind=kOutput, calls=%fused_computation.10 | convolution fusion | flops 8388608000 | bytes 26673152 | tf_op jit(solution)/shard_map/dot_general | solution.py:73
  (42 shorter events, 33.9 us)
Async XLA Ops:
  7.2 87.2 %all-gather.6.cloned.1.call-start = ((), (), s32[]{:S(2)}) async-start(), calls=%async_computation.6 | async-start | bytes 9437184 | tf_op jit(solution)/shard_map/all_gather | solution.py:40
  7.9 917.3 %reduce-scatter.3.cloned.1.call-start = ((), (), s32[]{:S(2)}) async-start(), calls=%async_computation.3 | async-start | bytes 20480000 | tf_op jit(solution)/shard_map/reduce_scatter | solution.py:50
  183.2 492.1 %copy-start.4 = (u32[32]{0:T(128)S(1)}, u32[32]{0:T(128)}, u32[]{:S(2)}) copy-start(u32[32]{0:T(128)} %constant.42) | copy-start | bytes 388
  183.3 876.8 %reduce-scatter.5.cloned.1.call-start = ((), (), s32[]{:S(2)}) async-start(), calls=%async_computation.4 | async-start | bytes 4718592 | tf_op jit(solution)/shard_map/reduce_scatter | solution.py:63
  183.3 310.7 %collective-permute-start = (bf16[1024,4000]{0,1:T(8,128)(2,1)}, bf16[1024,4000]{0,1:T(8,128)(2,1)S(1)}, u32[]{:S(2)}, u32[]{:S(2)}) collective-permute-start(bf16[1024,4000]{0,1:T(8,128)(2,1)} %param.7), channel_id=1, source_target_pairs={{0,8},{8,16},{16,24},{24,0},{1,9},{9,17},{17,25},{25,1},{2,10},{10... | collective-permute-start | bytes 24576008 | tf_op jit(solution)/shard_map/ppermute | solution.py:14
  494.0 3.3 copy-start.2
  497.3 178.0 %collective-permute-start.1 = (bf16[1024,4000]{0,1:T(8,128)(2,1)S(1)}, bf16[1024,4000]{0,1:T(8,128)(2,1)}, u32[]{:S(2)}, u32[]{:S(2)}) collective-permute-start(bf16[1024,4000]{0,1:T(8,128)(2,1)S(1)} %collective-permute-done), channel_id=1, source_target_pairs={{0,8},{8,16},{16,24},{24,0},{1,9},{9,17},{17,25},{25,1},{2,10},{10... | collective-permute-start | bytes 24576008 | tf_op jit(solution)/shard_map/ppermute | solution.py:14
  675.3 179.6 %collective-permute-start.2 = (bf16[1024,4000]{0,1:T(8,128)(2,1)}, bf16[1024,4000]{0,1:T(8,128)(2,1)}, u32[]{:S(2)}, u32[]{:S(2)}) collective-permute-start(bf16[1024,4000]{0,1:T(8,128)(2,1)} %collective-permute-done.1), channel_id=1, source_target_pairs={{0,8},{8,16},{16,24},{24,0},{1,9},{9,17},{17,25},{25,1},{2,10},{10... | collective-permute-start | bytes 24576008 | tf_op jit(solution)/shard_map/ppermute | solution.py:14
  862.4 15.2 %slice-start = ((s8[8192000]{0:T(1024)(128)(4,1)}), s8[4194304]{0:T(1024)(128)(4,1)S(1)}, s32[]{:S(2)}) async-start(s8[8192000]{0:T(1024)(128)(4,1)} %bitcast.35), calls=%async_computation.7 | async-start | bytes 8388608
  870.0 7.6 slice-start.1
  925.2 4.6 copy-start.1
  927.8 2.0 copy-start
  967.4 18.1 %copy-start.3 = (bf16[256,4000]{0,1:T(8,128)(2,1)}, bf16[256,4000]{0,1:T(8,128)(2,1)S(1)}, u32[]{:S(2)}) copy-start(bf16[256,4000]{0,1:T(8,128)(2,1)S(1)} %get-tuple-element.19) | copy-start | bytes 6144004
  985.6 134.9 %all-gather.4.cloned.1.call-start = ((), (), s32[]{:S(2)}) async-start(), calls=%async_computation.5 | async-start | bytes 10240000 | tf_op jit(solution)/shard_map/all_gather | solution.py:72
Sparse Core Ops, SparseCore 0:
  9.6 84.7 all-gather.5
  183.4 281.6 reduce-scatter.2
  985.7 48.3 reduce-scatter.4
  1035.9 84.5 all-gather.3
